TPU v7x, 32 devices: a whole 2x2x4 slice. The times are simulated.
32 devices in a mesh: expert: 16 (over z, y, x), dp: 2 (over core).
Axes of the slice: x: 2, y: 2, z: 4, core: 2. Of those that a mesh axis runs over, the one named last changes fastest.
Arguments:
- tokens: bfloat16 [2048, 2048], P(('expert', 'dp')), may hold values from -6 to 6
- expert_ids: int32 [2048, 8], P(('expert', 'dp')), may hold values from 0 to 15, all different within a row; in each aligned block of 64 rows (0 to 63, 64 to 127, ...) at most 48 rows name the same one
- gate_probs: float32 [2048, 8], P(('expert', 'dp')), may hold values from 0.05 to 1
- swap_flags: int32 [8], replicated, may hold values from 0 to 1, as said below
- w_gate: bfloat16 [16, 2048, 768], P('expert', 'dp'), may hold values from -0.125 to 0.125
- w_up: bfloat16 [16, 2048, 768], P('expert', 'dp'), may hold values from -0.125 to 0.125
- w_down: bfloat16 [16, 768, 2048], P('expert', None, 'dp'), may hold values from -0.21875 to 0.21875
Outputs:
- moe_out: bfloat16 [2048, 2048], P(('expert', 'dp'))
Inputs may be any that keep to these rules, and one draw needn't show every extreme that they name: `expert_ids`: each row names 8 different experts. Within the 64 rows of one device no expert is named by more than 48 rows, a bound that some block reaches. swap_flags[0] is 1; the other entries are 0 or 1.
All inputs are finite; a program needn't handle non-finite values.
Results may differ from a plain program's by a relative error of at most 0.0057.
Values may be sent and summed in bfloat16 or wider, within the bound.
A program may use at most 64 MiB of HBM per device.

v0:
```python
import jax
import jax.numpy as jnp
from jax import lax
from jax.sharding import PartitionSpec as P


def on_device(tokens, expert_ids, gate_probs, swap_flags, w_gate, w_up, w_down):
    axis_size = lax.axis_size("expert")
    own_index = lax.axis_index("expert")
    half_span = axis_size // 2
    shares = gate_probs / jnp.sum(gate_probs, axis=1, keepdims=True)
    experts = jnp.arange(axis_size, dtype=jnp.int32)
    dense = jnp.sum(
        jnp.where(expert_ids[:, :, None] == experts[None, None, :], shares[:, :, None], 0.0), axis=1
    )
    lower = own_index < half_span
    own_base = jnp.where(lower, own_index, own_index - half_span)
    own_flag = (
        jnp.sum(jnp.where(jnp.arange(half_span, dtype=jnp.int32) == own_base, swap_flags, 0)) == 1
    )
    served = jnp.where(
        own_flag, jnp.where(lower, own_index + half_span, own_index - half_span), own_index
    )
    rows = lax.all_gather(tokens, "expert", axis=0, tiled=True)
    dense_all = lax.all_gather(dense, "expert", axis=0, tiled=True)
    factor = jnp.sum(jnp.where(experts[None, :] == served, dense_all, 0.0), axis=1)
    gate_next = jnp.dot(
        rows,
        lax.all_gather(w_gate, "dp", axis=1, tiled=True)[0],
        preferred_element_type=jnp.float32,
    )
    up_next = jnp.dot(
        rows, lax.all_gather(w_up, "dp", axis=1, tiled=True)[0], preferred_element_type=jnp.float32
    )
    hidden = (jax.nn.silu(gate_next) * up_next).astype(jnp.bfloat16)
    produced = jnp.dot(
        hidden,
        lax.all_gather(w_down, "dp", axis=2, tiled=True)[0],
        preferred_element_type=jnp.float32,
    ).astype(jnp.bfloat16)
    partial = (factor[:, None] * produced.astype(jnp.float32)).astype(jnp.bfloat16)
    return lax.psum_scatter(partial, "expert", scatter_dimension=0, tiled=True)


def solution(mesh):
    placed = (
        P(("expert", "dp"), None),
        P(("expert", "dp"), None),
        P(("expert", "dp"), None),
        P(),
        P("expert", "dp", None),
        P("expert", "dp", None),
        P("expert", None, "dp"),
    )
    return jax.shard_map(
        on_device, mesh=mesh, in_specs=placed, out_specs=P(("expert", "dp"), None), check_vma=False
    )
```

profile of v0, /device:TPU:0, one launch (start us, length us, event | category | flops | bytes accessed | tf_op | source)
XLA Modules:
  0.0 246.6 jit_solution(10669585378727031929)
XLA Ops:
  6.5 0.0 all-gather.10.cloned.1.call-start
  6.5 0.7 all-gather.10.cloned.1.call-update
  7.3 0.0 all-gather.6.cloned.1.call-start
  7.3 0.7 all-gather.6.cloned.1.call-update
  8.0 0.0 all-gather.8.cloned.1.call-start
  8.1 0.7 all-gather.8.cloned.1.call-update
  8.7 0.0 all-gather.12.cloned.1.call-start
  8.8 0.5 all-gather.12.cloned.1.call-update
  9.3 0.0 reduce-scatter.2.cloned.1.call-start
  9.4 0.0 copy-done
  9.4 0.0 copy-done.1
  9.5 43.1 %all-gather = f32[16,64,16]{1,2,0:T(8,128)S(1)} all-gather(f32[1,64,16]{1,2,0:T(8,128)S(1)} %bitcast.18), channel_id=1, replica_groups=mesh['expert'=16,'dp'=2] {'expert'}, dimensions={0}, use_global_device_ids=true | all-gather | bytes 69632 | tf_op jit(solution)/shard_map/all_gather | solution.py:25
  52.6 0.1 reshape.10
  52.7 0.0 copy-done.2
  52.7 0.6 fusion.9
  54.0 0.1 select_reduce_fusion
  54.1 0.0 all-gather.10.cloned.1.call-done
  54.1 49.5 %all-gather.6.cloned.1.call-done = bf16[1024,2048]{1,0:T(8,128)(2,1)} async-done(((bf16[64,2048]{1,0:T(8,128)(2,1)}), bf16[1024,2048]{1,0:T(8,128)(2,1)}) %all-gather.6.cloned.1.call-update) | async-done | bytes 4194320 | tf_op jit(solution)/shard_map/all_gather | solution.py:24
  103.7 6.1 %fusion.1 = f32[1024,768]{1,0:T(8,128)S(1)} fusion(bf16[1024,2048]{1,0:T(8,128)(2,1)} %all-gather.6.cloned.1.call-done, bf16[1,2048,768]{2,1,0:T(8,128)(2,1)} %all-gather.10.cloned.1.call-done), kind=kOutput, calls=%fused_computation.2 | convolution fusion | flops 3221225472 | bytes 10485760 | tf_op jit(solution)/shard_map/dot_general | solution.py:32
  109.8 6.2 %all-gather.8.cloned.1.call-done = bf16[1,2048,768]{2,1,0:T(8,128)(2,1)} async-done(((bf16[1,1024,768]{2,1,0:T(8,128)(2,1)}), bf16[1,2048,768]{2,1,0:T(8,128)(2,1)}) %all-gather.8.cloned.1.call-update) | async-done | bytes 3145744 | tf_op jit(solution)/shard_map/all_gather | solution.py:29
  116.0 14.7 %all-gather.12.cloned.1.call-done = bf16[1,768,2048]{2,1,0:T(8,128)(2,1)} async-done(((bf16[1,768,1024]{2,1,0:T(8,128)(2,1)}), bf16[1,768,2048]{2,1,0:T(8,128)(2,1)}) %all-gather.12.cloned.1.call-update) | async-done | bytes 3145744 | tf_op jit(solution)/shard_map/all_gather | solution.py:38
  130.7 12.8 %multiply_convert_fusion = bf16[1024,2048]{1,0:T(8,128)(2,1)} fusion(f32[1024]{0:T(1024)S(1)} %select_reduce_fusion, bf16[1,768,2048]{2,1,0:T(8,128)(2,1)} %all-gather.12.cloned.1.call-done, f32[1024,768]{1,0:T(8,128)S(1)} %fusion.1, bf16[1024,2048]{1,0:T(8,128)(2,1)} %all-gather.6.cloned.1.call-done, bf16[1,2048,768]{2,1,0:T(8,128)(2,1)} %all-gather.8.cloned.1.call-done), kind=kOutput, calls=%fused_computation | convolution fusion | flops 6455558144 | bytes 17829888 | tf_op jit(solution)/shard_map/dot_general | solution.py:36
  143.5 0.0 reduce-scatter.2.cloned.1.call-update
  143.6 96.5 %reduce-scatter.2.cloned.1.call-done = bf16[64,2048]{1,0:T(8,128)(2,1)} async-done(((bf16[1024,2048]{1,0:T(8,128)(2,1)}), bf16[64,2048]{1,0:T(8,128)(2,1)}) %reduce-scatter.2.cloned.1.call-update) | async-done | bytes 262160 | tf_op jit(solution)/shard_map/reduce_scatter | solution.py:42
  (8 shorter events, 0.1 us)
Async XLA Ops:
  6.5 2.8 %copy-start = (f32[64,8]{0,1:T(8,128)S(1)}, f32[64,8]{0,1:T(8,128)}, u32[]{:S(2)}) copy-start(f32[64,8]{0,1:T(8,128)} %param.9) | copy-start | bytes 6148
  6.5 2.9 %copy-start.1 = (s32[64,8]{0,1:T(8,128)S(1)}, s32[64,8]{0,1:T(8,128)}, u32[]{:S(2)}) copy-start(s32[64,8]{0,1:T(8,128)} %param.8) | copy-start | bytes 6148
  6.5 46.2 %copy-start.2 = (s32[8]{0:T(128)S(1)}, s32[8]{0:T(128)}, u32[]{:S(2)}) copy-start(s32[8]{0:T(128)} %param.10) | copy-start | bytes 100
  6.5 47.6 %all-gather.10.cloned.1.call-start = ((), (), s32[]{:S(2)}) async-start(), calls=%async_computation.3 | async-start | bytes 4718592 | tf_op jit(solution)/shard_map/all_gather | solution.py:33
  7.3 96.4 %all-gather.6.cloned.1.call-start = ((), (), s32[]{:S(2)}) async-start(), calls=%async_computation.1 | async-start | bytes 4456448 | tf_op jit(solution)/shard_map/all_gather | solution.py:24
  8.0 108.0 %all-gather.8.cloned.1.call-start = ((), (), s32[]{:S(2)}) async-start(), calls=%async_computation.2 | async-start | bytes 4718592 | tf_op jit(solution)/shard_map/all_gather | solution.py:29
  8.7 121.9 %all-gather.12.cloned.1.call-start = ((), (), s32[]{:S(2)}) async-start(), calls=%async_computation.4 | async-start | bytes 4718592 | tf_op jit(solution)/shard_map/all_gather | solution.py:38
  9.3 230.7 %reduce-scatter.2.cloned.1.call-start = ((), (), s32[]{:S(2)}) async-start(), calls=%async_computation.5 | async-start | bytes 4456448 | tf_op jit(solution)/shard_map/reduce_scatter | solution.py:42
Sparse Core Ops, SparseCore 0:
  8.9 14.8 all-gather.9
  26.5 77.0 all-gather.5
  105.2 10.7 all-gather.7
  117.4 13.2 all-gather.11
  143.7 96.3 reduce-scatter.1
where the time goes:
time: 247 us
  waiting for transfers between devices  170 us (69%)
  blocking collectives  43.1 us (17%)
  matrix products  19 us (8%)
  between operations  13.9 us (6%)
    reduce_scatter x1, waiting for transfers between devices, on_device(): return lax.psum_scatter(partial, 'expert', scatter_dimension=0, tiled=True)  96.5 us
    all_gather x1, waiting for transfers between devices, on_device(): rows = lax.all_gather(tokens, 'expert', axis=0, tiled=True)  49.5 us
    all_gather x1, blocking collectives, on_device(): dense_all = lax.all_gather(dense, 'expert', axis=0, tiled=True)  43.1 us
    all_gather x1, waiting for transfers between devices, on_device(): lax.all_gather(w_down, 'dp', axis=2, tiled=True)[0]  14.7 us
    dot_general x1, matrix products, on_device(): jnp.dot(hidden, lax.all_gather(w_down, 'dp', axis=2, tiled=True)[0], pref...  12.8 us
    all_gather x1, waiting for transfers between devices, on_device(): lax.all_gather(w_gate, 'dp', axis=1, tiled=True)[0]  6.18 us
    dot_general x1, matrix products, on_device(): jnp.dot(rows, lax.all_gather(w_up, 'dp', axis=1, tiled=True)[0], preferre...  6.12 us
  transfers between devices with their start and end apart: 5, of which 4 were waited for; matrix products, arithmetic and copies ran while one was open for 3% of the time, Pallas kernels for 0%

commit v1 on v0

--- a/solution.py
+++ b/solution.py
@@ -21,8 +21,13 @@
     served = jnp.where(
         own_flag, jnp.where(lower, own_index + half_span, own_index - half_span), own_index
     )
-    rows = lax.all_gather(tokens, "expert", axis=0, tiled=True)
-    dense_all = lax.all_gather(dense, "expert", axis=0, tiled=True)
+
+    def records_start(local_array, local_x, axis_key):
+        seen_now = jnp.concatenate([local_array, local_x], axis=1)
+        shaped = lax.all_gather(seen_now, axis_name=axis_key, axis=0, tiled=True)
+        return jnp.split(shaped, [local_array.shape[1]], axis=1)
+
+    rows, dense_all = records_start(tokens, dense, "expert")
     factor = jnp.sum(jnp.where(experts[None, :] == served, dense_all, 0.0), axis=1)
     gate_next = jnp.dot(
         rows,

time: 247 us -> 289 us (1.17)
  waiting for transfers between devices: 170 us -> 249 us
  blocking collectives: 43.1 us -> 0 us
  other arithmetic: 0.77 us -> 5.81 us
    all_gather x1, waiting for transfers between devices: 49.5 us -> 117 us  [records_start(): shaped = lax.all_gather(seen_now, axis_name=axis_key, axis=0, tiled=True)]
    all_gather x1 -> x0, blocking collectives: 43.1 us -> none  [on_device(): dense_all = lax.all_gather(dense, 'expert', axis=0, tiled=True)]
    all_gather x1, waiting for transfers between devices: 0.02 us -> 8.1 us  [on_device(): lax.all_gather(w_up, 'dp', axis=1, tiled=True)[0]]
    all_gather x1, waiting for transfers between devices: 6.18 us -> 10.6 us  [on_device(): lax.all_gather(w_gate, 'dp', axis=1, tiled=True)[0]]
  transfers between devices with their start and end apart: 5 -> 5, of which waited for: 4 -> 5; matrix products, arithmetic and copies ran while one was open for 3% -> 3% of each run, Pallas kernels for 0% -> 0%
where the time goes in v1:
time: 289 us
  waiting for transfers between devices  249 us (86%)
  matrix products  20.2 us (7%)
  between operations  13.8 us (5%)
  other arithmetic  5.81 us (2%)
    all_gather x1, waiting for transfers between devices, records_start(): shaped = lax.all_gather(seen_now, axis_name=axis_key, axis=0, tiled=True)  117 us
    reduce_scatter x1, waiting for transfers between devices, on_device(): return lax.psum_scatter(partial, 'expert', scatter_dimension=0, tiled=True)  96.4 us
    all_gather x1, waiting for transfers between devices, on_device(): lax.all_gather(w_down, 'dp', axis=2, tiled=True)[0]  14.7 us
    dot_general x1, matrix products, on_device(): jnp.dot(hidden, lax.all_gather(w_down, 'dp', axis=2, tiled=True)[0], pref...  13.4 us
    all_gather x1, waiting for transfers between devices, on_device(): lax.all_gather(w_gate, 'dp', axis=1, tiled=True)[0]  10.6 us
    all_gather x1, waiting for transfers between devices, on_device(): lax.all_gather(w_up, 'dp', axis=1, tiled=True)[0]  8.1 us
    dot_general x1, matrix products, on_device(): jnp.dot(rows, lax.all_gather(w_gate, 'dp', axis=1, tiled=True)[0], prefer...  6.77 us
  transfers between devices with their start and end apart: 5, of which 5 were waited for; matrix products, arithmetic and copies ran while one was open for 3% of the time, Pallas kernels for 0%

profile of v1, /device:TPU:0, one launch (start us, length us, event | category | flops | bytes accessed | tf_op | source)
XLA Modules:
  0.0 289.1 jit_solution(15684480819451755601)
XLA Ops:
  6.5 0.7 reduce_sum.37
  7.2 0.7 broadcast_divide_fusion
  7.9 0.7 select_reduce_fusion
  8.6 0.1 copy.10
  8.7 1.0 convert_element_type.15
  9.7 0.8 pad_maximum_fusion
  10.6 0.0 all-gather.5.cloned.1.call-update
  10.6 0.0 all-gather.7.cloned.1.call-start
  10.6 0.7 all-gather.7.cloned.1.call-update
  11.3 0.0 all-gather.9.cloned.1.call-start
  11.4 0.7 all-gather.9.cloned.1.call-update
  12.1 0.0 all-gather.11.cloned.1.call-start
  12.1 0.5 all-gather.11.cloned.1.call-update
  12.7 0.0 reduce-scatter.2.cloned.1.call-start
  12.7 0.6 fusion.16
  14.0 117.1 %all-gather.5.cloned.1.call-done = f32[1024,2064]{1,0:T(8,128)} async-done(((f32[64,2064]{1,0:T(8,128)}), f32[1024,2064]{1,0:T(8,128)}) %all-gather.5.cloned.1.call-update) | async-done | bytes 8454160 | tf_op jit(solution)/shard_map/all_gather | solution.py:27
  131.2 1.2 fusion.15
  132.4 10.6 %all-gather.7.cloned.1.call-done = bf16[1,2048,768]{2,1,0:T(8,128)(2,1)} async-done(((bf16[1,1024,768]{2,1,0:T(8,128)(2,1)}), bf16[1,2048,768]{2,1,0:T(8,128)(2,1)}) %all-gather.7.cloned.1.call-update) | async-done | bytes 3145744 | tf_op jit(solution)/shard_map/all_gather | solution.py:34
  143.1 6.8 %fusion.2 = f32[1024,768]{1,0:T(8,128)S(1)} fusion(f32[1024,2064]{1,0:T(8,128)} %all-gather.5.cloned.1.call-done, bf16[1,2048,768]{2,1,0:T(8,128)(2,1)} %all-gather.7.cloned.1.call-done), kind=kOutput, calls=%fused_computation.3 | convolution fusion | flops 3221225472 | bytes 10485760 | tf_op jit(solution)/shard_map/dot_general | solution.py:32
  149.8 8.1 %all-gather.9.cloned.1.call-done = bf16[1,2048,768]{2,1,0:T(8,128)(2,1)} async-done(((bf16[1,1024,768]{2,1,0:T(8,128)(2,1)}), bf16[1,2048,768]{2,1,0:T(8,128)(2,1)}) %all-gather.9.cloned.1.call-update) | async-done | bytes 3145744 | tf_op jit(solution)/shard_map/all_gather | solution.py:38
  157.9 14.7 %all-gather.11.cloned.1.call-done = bf16[1,768,2048]{2,1,0:T(8,128)(2,1)} async-done(((bf16[1,768,1024]{2,1,0:T(8,128)(2,1)}), bf16[1,768,2048]{2,1,0:T(8,128)(2,1)}) %all-gather.11.cloned.1.call-update) | async-done | bytes 3145744 | tf_op jit(solution)/shard_map/all_gather | solution.py:43
  172.7 13.4 %multiply_convert_fusion = bf16[1024,2048]{1,0:T(8,128)(2,1)} fusion(f32[1024]{0:T(1024)S(1)} %fusion.15, bf16[1,768,2048]{2,1,0:T(8,128)(2,1)} %all-gather.11.cloned.1.call-done, f32[1024,768]{1,0:T(8,128)S(1)} %fusion.2, bf16[1,2048,768]{2,1,0:T(8,128)(2,1)} %all-gather.9.cloned.1.call-done, f32[1024,2064]{1,0:T(8,128)} %all-gather.5.cloned.1.call-done), kind=kOutput, calls=%fused_computation | convolution fusion | flops 6455558144 | bytes 17829888 | tf_op jit(solution)/shard_map/dot_general | solution.py:41
  186.1 0.0 reduce-scatter.2.cloned.1.call-update
  186.1 96.4 %reduce-scatter.2.cloned.1.call-done = bf16[64,2048]{1,0:T(8,128)(2,1)} async-done(((bf16[1024,2048]{1,0:T(8,128)(2,1)}), bf16[64,2048]{1,0:T(8,128)(2,1)}) %reduce-scatter.2.cloned.1.call-update) | async-done | bytes 262160 | tf_op jit(solution)/shard_map/reduce_scatter | solution.py:47
  (4 shorter events, 0.0 us)
Async XLA Ops:
  6.5 124.6 %all-gather.5.cloned.1.call-start = ((), (), s32[]{:S(2)}) async-start(), calls=%async_computation.1 | async-start | bytes 9469952 | tf_op jit(solution)/shard_map/all_gather | solution.py:27
  9.7 3.0 %copy-start = (s32[8]{0:T(128)S(1)}, s32[8]{0:T(128)}, u32[]{:S(2)}) copy-start(s32[8]{0:T(128)} %param.10) | copy-start | bytes 100
  10.6 132.5 %all-gather.7.cloned.1.call-start = ((), (), s32[]{:S(2)}) async-start(), calls=%async_computation.2 | async-start | bytes 4718592 | tf_op jit(solution)/shard_map/all_gather | solution.py:34
  11.3 146.6 %all-gather.9.cloned.1.call-start = ((), (), s32[]{:S(2)}) async-start(), calls=%async_computation.3 | async-start | bytes 4718592 | tf_op jit(solution)/shard_map/all_gather | solution.py:38
  12.1 160.6 %all-gather.11.cloned.1.call-start = ((), (), s32[]{:S(2)}) async-start(), calls=%async_computation.4 | async-start | bytes 4718592 | tf_op jit(solution)/shard_map/all_gather | solution.py:43
  12.7 269.9 %reduce-scatter.2.cloned.1.call-start = ((), (), s32[]{:S(2)}) async-start(), calls=%async_computation.5 | async-start | bytes 4456448 | tf_op jit(solution)/shard_map/reduce_scatter | solution.py:47
Sparse Core Ops, SparseCore 0:
  10.7 120.4 all-gather.4
  132.7 10.3 all-gather.6
  144.6 13.2 all-gather.8
  159.3 13.2 all-gather.10
  186.2 96.2 reduce-scatter.1
